TPU v7x, 256 devices: a whole 4x4x8 slice. The times are simulated.
256 devices in a mesh: row: 8 (over x, y_lo), col: 32 (over y_hi, z, core).
Axes of the slice: x: 4, y: 4 (y_hi: 2, y_lo: 2; y = y_hi * 2 + y_lo), z: 8, core: 2. Of those that a mesh axis runs over, the one named last changes fastest.
Arguments:
- features: bfloat16 [65536, 128], P(('row', 'col')), may hold values from -6 to 6
- degrees: int32 [65536], P(('row', 'col')), may hold values from 32 to 159
- adj_tiles: bfloat16 [8, 32, 256, 4096], P('row', 'col'), may hold values from 0 to 0.22472483, as said below
- tile_rows: int32 [8, 32, 256], P('row', 'col'), may hold values from 0 to 127
- tile_cols: int32 [8, 32, 256], P('row', 'col'), may hold values from 0 to 31
- tile_counts: int32 [8, 32], P('row', 'col'), may hold values from 64 to 256, as said below
Outputs:
- propagated: bfloat16 [65536, 128], P(('row', 'col'))
Inputs may be any that keep to these rules, and one draw needn't show every extreme that they name: Each block holds at most 256 live tiles, in its first tile_counts slots; some block holds exactly 256. `adj_tiles`: edge weights are zero or positive.
All inputs are finite; a program needn't handle non-finite values.
Results may differ from a plain program's by a relative error of at most 0.0054.
Values may be sent and summed in bfloat16 or wider, within the bound.
A program may use at most 128 MiB of HBM per device.

v0:
```python
import jax
import jax.numpy as jnp
from jax import lax
from jax.sharding import PartitionSpec as P

TILE = 64
KNN = 32
STEPS = 2
ALPHA = 0.1


def shards(features, degrees, adj_tiles, tile_rows, tile_cols, tile_counts):
    col_count = lax.axis_size("col")
    nodes_dev = features.shape[0]
    feat_width = features.shape[1]
    tile_slots = adj_tiles.shape[2]
    dev_tiles = adj_tiles.reshape(tile_slots, TILE, TILE)
    row_ids_all = tile_rows.reshape(tile_slots)
    col_ids_all = tile_cols.reshape(tile_slots)
    live_count = tile_counts.reshape(())
    block_len = min(256, tile_slots)
    num_turns = tile_slots // block_len
    row_tiles = nodes_dev * col_count // TILE
    norm_scale = jnp.sqrt(KNN / degrees.astype(jnp.float32))[:, None]
    teleport = ALPHA * features.astype(jnp.float32)
    current = features.astype(jnp.float32)
    for repeat in range(STEPS):
        source = (norm_scale * current).astype(jnp.bfloat16)
        col_panel = lax.all_gather(source, "row", axis=0, tiled=True).reshape(-1, TILE, feat_width)

        def add_block(turn_index, totals):
            first_tile = turn_index * block_len
            live_mask = first_tile + jnp.arange(block_len, dtype=jnp.int32) < live_count
            inputs = col_panel[col_ids_all]
            products = jnp.einsum(
                "tab,tbf->taf", dev_tiles, inputs, preferred_element_type=jnp.float32
            )
            products = jnp.where(live_mask[:, None, None], products, jnp.zeros_like(products))
            return totals.at[row_ids_all].add(products)

        start_tot = jnp.zeros((row_tiles, TILE, feat_width), jnp.float32)
        totals = lax.fori_loop(0, num_turns, add_block, start_tot)
        partial_rows = totals.reshape(row_tiles * TILE, feat_width)
        own_rows = lax.psum_scatter(partial_rows, "col", scatter_dimension=0, tiled=True)
        current = (1.0 - ALPHA) * norm_scale * own_rows + teleport
    return current.astype(jnp.bfloat16)


def solution(mesh):
    return jax.shard_map(
        shards,
        mesh=mesh,
        in_specs=(
            P(("row", "col"), None),
            P(("row", "col")),
            P("row", "col", None, None),
            P("row", "col", None),
            P("row", "col", None),
            P("row", "col"),
        ),
        out_specs=P(("row", "col"), None),
        check_vma=False,
    )
```

profile of v0, /device:TPU:6, one launch (start us, length us, event | category | flops | bytes accessed | tf_op | source)
XLA Modules:
  0.0 449.4 jit_solution(6399208129320878904)
XLA Ops:
  6.5 0.0 reduce-scatter.3.cloned.1.call-start
  7.2 0.7 compare_select_fusion.1
  7.9 0.7 compare_select_fusion
  8.6 0.7 broadcast_multiply_fusion
  9.3 0.9 fusion.5
  10.2 28.9 %all_gather.6 = bf16[2048,128]{1,0:T(8,128)(2,1)S(1)} all-gather(bf16[256,128]{1,0:T(8,128)(2,1)S(1)} %fusion.5), channel_id=1, replica_groups=mesh['row'=8,'col'=32] {'row'}, dimensions={0}, use_global_device_ids=true | all-gather | bytes 589824 | tf_op jit(solution)/shard_map/all_gather | solution.py:29
  39.1 3.3 copy.7
  42.4 6.6 %copy.8 = bf16[256,64,64]{2,1,0:T(8,128)(2,1)} copy(bf16[256,64,64]{0,2,1:T(8,128)(2,1)S(1)} %bitcast.25) | data formatting | bytes 4194304 | tf_op jit(solution)/shard_map/reshape | solution.py:17
  49.0 3.0 gather_fusion
  52.1 7.9 %select_bitcast_fusion.1 = f32[256,64,128]{2,1,0:T(8,128)} fusion(pred[256]{0:T(512)(128)(4,1)S(1)} %iota_compare_fusion, bf16[256,64,64]{2,1,0:T(8,128)(2,1)} %copy.8, bf16[256,64,128]{2,1,0:T(8,128)(2,1)} %gather_fusion), kind=kOutput, calls=%fused_computation.5 | convolution fusion | flops 270532608 | bytes 14680320 | tf_op jit(solution)/shard_map/while/body/eval_jaxpr/tab,tbf->taf/dot_general | solution.py:35
  60.0 2.5 broadcast.71.clone
  62.5 39.3 %scatter_fusion = f32[128,64,128]{2,1,0:T(8,128)} fusion(f32[128,64,128]{2,1,0:T(8,128)} %broadcast.71.clone, s32[256]{0:T(256)S(1)} %bitcast.26, f32[256,64,128]{2,1,0:T(8,128)} %select_bitcast_fusion.1), kind=kCustom, calls=%fused_computation.2 | custom fusion | flops 2097152 | bytes 25166848 | tf_op jit(solution)/shard_map/while/body/eval_jaxpr/scatter-add | solution.py:39
  101.8 0.0 copy-start
  101.8 0.0 reduce-scatter.3.cloned.1.call-update
  101.8 0.0 reduce-scatter.5.cloned.1.call-start
  101.9 130.7 %reduce-scatter.3.cloned.1.call-done = f32[256,128]{1,0:T(8,128)} async-done(((f32[8192,128]{1,0:T(8,128)}), f32[256,128]{1,0:T(8,128)}) %reduce-scatter.3.cloned.1.call-update) | async-done | bytes 131088 | tf_op jit(solution)/shard_map/reduce_scatter | solution.py:44
  232.6 0.0 copy-done
  232.6 1.0 fusion.3
  233.6 26.8 %all_gather.7 = bf16[2048,128]{1,0:T(8,128)(2,1)S(1)} all-gather(bf16[256,128]{1,0:T(8,128)(2,1)S(1)} %fusion.3), channel_id=1, replica_groups=mesh['row'=8,'col'=32] {'row'}, dimensions={0}, use_global_device_ids=true | all-gather | bytes 589824 | tf_op jit(solution)/shard_map/all_gather | solution.py:29
  260.4 3.0 gather_fusion.1
  263.4 7.9 %select_bitcast_fusion = f32[256,64,128]{2,1,0:T(8,128)} fusion(pred[256]{0:T(512)(128)(4,1)S(1)} %iota_compare_fusion, bf16[256,64,64]{2,1,0:T(8,128)(2,1)} %copy.8, bf16[256,64,128]{2,1,0:T(8,128)(2,1)} %gather_fusion.1), kind=kOutput, calls=%fused_computation.4 | convolution fusion | flops 270532608 | bytes 14680320 | tf_op jit(solution)/shard_map/while/body/eval_jaxpr/tab,tbf->taf/dot_general | solution.py:35
  271.3 2.5 broadcast.71
  273.8 39.3 %scatter_fusion.1 = f32[128,64,128]{2,1,0:T(8,128)} fusion(f32[128,64,128]{2,1,0:T(8,128)} %broadcast.71, s32[256]{0:T(256)S(1)} %bitcast.27, f32[256,64,128]{2,1,0:T(8,128)} %select_bitcast_fusion), kind=kCustom, calls=%fused_computation.3 | custom fusion | flops 2097152 | bytes 25166848 | tf_op jit(solution)/shard_map/while/body/eval_jaxpr/scatter-add | solution.py:39
  313.2 0.0 reduce-scatter.5.cloned.1.call-update
  313.2 127.7 %reduce-scatter.5.cloned.1.call-done = f32[256,128]{1,0:T(8,128)} async-done(((f32[8192,128]{1,0:T(8,128)}), f32[256,128]{1,0:T(8,128)}) %reduce-scatter.5.cloned.1.call-update) | async-done | bytes 131088 | tf_op jit(solution)/shard_map/reduce_scatter | solution.py:44
  440.9 1.6 fusion.4
  (2 shorter events, 0.0 us)
Async XLA Ops:
  6.5 226.0 %reduce-scatter.3.cloned.1.call-start = ((), (), s32[]{:S(2)}) async-start(), calls=%async_computation.2 | async-start | bytes 4325376 | tf_op jit(solution)/shard_map/reduce_scatter | solution.py:44
  101.8 130.8 %copy-start = (bf16[256,128]{1,0:T(8,128)(2,1)S(1)}, bf16[256,128]{1,0:T(8,128)(2,1)}, u32[]{:S(2)}) copy-start(bf16[256,128]{1,0:T(8,128)(2,1)} %param.6) | copy-start | bytes 196612
  101.8 339.1 %reduce-scatter.5.cloned.1.call-start = ((), (), s32[]{:S(2)}) async-start(), calls=%async_computation.3 | async-start | bytes 4325376 | tf_op jit(solution)/shard_map/reduce_scatter | solution.py:44
Sparse Core Ops, SparseCore 0:
  101.9 130.5 reduce-scatter.2
  313.3 127.5 reduce-scatter.4
where the time goes:
time: 451 us; the launch traced here: 449 us
  waiting for transfers between devices  258 us (57%)
  other arithmetic  84.3 us (19%)
  blocking collectives  55.6 us (12%)
  local copies, waits for them, and re-layouts  21 us (5%)
  matrix products  15.9 us (4%)
  between operations  14.1 us (3%)
    reduce_scatter x2, waiting for transfers between devices, shards(): lax.psum_scatter(partial_rows, 'col', scatter_dimension=0, tiled=True)  258 us
    scatter-add x2, other arithmetic, add_block(): return totals.at[row_ids_all].add(products)  78.6 us
    all_gather x2, blocking collectives, shards(): lax.all_gather(source, 'row', axis=0, tiled=True)  55.6 us
    dot_general x2, matrix products, add_block(): jnp.einsum('tab,tbf->taf', dev_tiles, inputs, preferred_element_type=jnp....  15.9 us
  transfers between devices with their start and end apart: 2, of which 2 were waited for; matrix products, arithmetic and copies ran while one was open for 0% of the time, Pallas kernels for 0%

commit v1 on v0

--- a/solution.py
+++ b/solution.py
@@ -26,7 +26,16 @@
     current = features.astype(jnp.float32)
     for repeat in range(STEPS):
         source = (norm_scale * current).astype(jnp.bfloat16)
-        col_panel = lax.all_gather(source, "row", axis=0, tiled=True).reshape(-1, TILE, feat_width)
+        _wrap_view = lambda w_in: jnp.concatenate(
+            lax.all_to_all(
+                jnp.stack(lax.axis_size("row") * [w_in], 0),
+                axis_name="row",
+                split_axis=0,
+                concat_axis=0,
+            ),
+            0,
+        )
+        col_panel = _wrap_view(source).reshape(-1, TILE, feat_width)
 
         def add_block(turn_index, totals):
             first_tile = turn_index * block_len

time: 451 us -> 411 us (0.911)
  blocking collectives: 55.6 us -> 10.9 us
  starting transfers between devices: 0.04 us -> 5.83 us
    all_gather x2 -> x0, blocking collectives: 55.6 us -> none  [shards(): lax.all_gather(source, 'row', axis=0, tiled=True)]
    all_to_all x0 -> x1, blocking collectives: none -> 10.9 us  [shards(): lax.all_to_all(jnp.stack(lax.axis_size('row') * [w_in], 0), axis_name='ro...]
    all_to_all x0 -> x1, starting transfers between devices: none -> 5.79 us  [shards(): lax.all_to_all(jnp.stack(lax.axis_size('row') * [w_in], 0), axis_name='ro...]
  transfers between devices with their start and end apart: 2 -> 3, of which waited for: 2 -> 2; matrix products, arithmetic and copies ran while one was open for 0% -> 3% of each run, Pallas kernels for 0% -> 0%
where the time goes in v1:
time: 411 us; the launch traced here: 410 us
  waiting for transfers between devices  257 us (63%)
  other arithmetic  83.6 us (20%)
  local copies, waits for them, and re-layouts  21.9 us (5%)
  matrix products  15.9 us (4%)
  between operations  14.1 us (3%)
  blocking collectives  10.9 us (3%)
  starting transfers between devices  5.83 us (1%)
    reduce_scatter x2, waiting for transfers between devices, shards(): lax.psum_scatter(partial_rows, 'col', scatter_dimension=0, tiled=True)  257 us
    scatter-add x2, other arithmetic, add_block(): return totals.at[row_ids_all].add(products)  78.6 us
    dot_general x2, matrix products, add_block(): jnp.einsum('tab,tbf->taf', dev_tiles, inputs, preferred_element_type=jnp....  15.9 us
    all_to_all x1, blocking collectives, shards(): lax.all_to_all(jnp.stack(lax.axis_size('row') * [w_in], 0), axis_name='ro...  10.9 us
  transfers between devices with their start and end apart: 3, of which 2 were waited for; matrix products, arithmetic and copies ran while one was open for 3% of the time, Pallas kernels for 0%

profile of v1, /device:TPU:6, one launch (start us, length us, event | category | flops | bytes accessed | tf_op | source)
XLA Modules:
  0.0 409.5 jit_solution(1624326774405366969)
XLA Ops:
  6.5 0.7 broadcast_multiply_fusion
  7.2 0.9 fusion.5
  8.2 0.9 stack.4
  9.0 5.8 %all-to-all-start = ((bf16[8,256,128]{2,1,0:T(8,128)(2,1)}), bf16[8,256,128]{2,1,0:T(8,128)(2,1)S(1)}, u32[]{:S(2)}, u32[]{:S(2)}) async-start(bf16[8,256,128]{2,1,0:T(8,128)(2,1)} %stack.4), calls=%async_computation | async-start | bytes 1048576 | tf_op jit(solution)/shard_map/all_to_all | solution.py:30
  14.8 0.0 reduce-scatter.3.cloned.1.call-start
  14.8 0.7 compare_select_fusion
  16.2 3.3 copy.7
  19.4 0.0 copy-start.1
  19.5 6.6 %copy.8 = bf16[256,64,64]{2,1,0:T(8,128)(2,1)} copy(bf16[256,64,64]{0,2,1:T(8,128)(2,1)S(1)} %bitcast.25) | data formatting | bytes 4194304 | tf_op jit(solution)/shard_map/reshape | solution.py:17
  26.1 0.0 copy-done.1
  26.1 0.0 all-to-all-done
  26.1 3.1 gather_fusion
  29.2 7.9 %select_bitcast_fusion.1 = f32[256,64,128]{2,1,0:T(8,128)} fusion(pred[256]{0:T(512)(128)(4,1)S(1)} %iota_compare_fusion, bf16[256,64,64]{2,1,0:T(8,128)(2,1)} %copy.8, bf16[256,64,128]{2,1,0:T(8,128)(2,1)} %gather_fusion), kind=kOutput, calls=%fused_computation.5 | convolution fusion | flops 270532608 | bytes 14680320 | tf_op jit(solution)/shard_map/while/body/eval_jaxpr/tab,tbf->taf/dot_general | solution.py:44
  37.1 2.5 broadcast.75.clone
  39.6 39.3 %scatter_fusion = f32[128,64,128]{2,1,0:T(8,128)} fusion(f32[128,64,128]{2,1,0:T(8,128)} %broadcast.75.clone, s32[256]{0:T(256)S(1)} %bitcast.26, f32[256,64,128]{2,1,0:T(8,128)} %select_bitcast_fusion.1), kind=kCustom, calls=%fused_computation.2 | custom fusion | flops 2097152 | bytes 25166848 | tf_op jit(solution)/shard_map/while/body/eval_jaxpr/scatter-add | solution.py:48
  78.9 0.0 copy-start
  78.9 0.0 reduce-scatter.3.cloned.1.call-update
  78.9 0.0 reduce-scatter.5.cloned.1.call-start
  79.0 130.5 %reduce-scatter.3.cloned.1.call-done = f32[256,128]{1,0:T(8,128)} async-done(((f32[8192,128]{1,0:T(8,128)}), f32[256,128]{1,0:T(8,128)}) %reduce-scatter.3.cloned.1.call-update) | async-done | bytes 131088 | tf_op jit(solution)/shard_map/reduce_scatter | solution.py:53
  209.5 0.0 copy-done
  209.5 1.0 fusion.3
  210.6 0.1 stack.5
  210.6 10.9 %all_to_all.10 = bf16[8,256,128]{2,1,0:T(8,128)(2,1)S(1)} all-to-all(bf16[8,256,128]{2,1,0:T(8,128)(2,1)S(1)} %stack.5), channel_id=1, replica_groups=mesh['row'=8,'col'=32] {'row'}, dimensions={0} | all-to-all | bytes 1048576 | tf_op jit(solution)/shard_map/all_to_all | solution.py:30
  221.5 3.0 gather_fusion.1
  224.6 7.9 %select_bitcast_fusion = f32[256,64,128]{2,1,0:T(8,128)} fusion(pred[256]{0:T(512)(128)(4,1)S(1)} %iota_compare_fusion, bf16[256,64,64]{2,1,0:T(8,128)(2,1)} %copy.8, bf16[256,64,128]{2,1,0:T(8,128)(2,1)} %gather_fusion.1), kind=kOutput, calls=%fused_computation.4 | convolution fusion | flops 270532608 | bytes 14680320 | tf_op jit(solution)/shard_map/while/body/eval_jaxpr/tab,tbf->taf/dot_general | solution.py:44
  232.5 2.5 broadcast.75
  235.0 39.3 %scatter_fusion.1 = f32[128,64,128]{2,1,0:T(8,128)} fusion(f32[128,64,128]{2,1,0:T(8,128)} %broadcast.75, s32[256]{0:T(256)S(1)} %bitcast.27, f32[256,64,128]{2,1,0:T(8,128)} %select_bitcast_fusion), kind=kCustom, calls=%fused_computation.3 | custom fusion | flops 2097152 | bytes 25166848 | tf_op jit(solution)/shard_map/while/body/eval_jaxpr/scatter-add | solution.py:48
  274.3 0.0 reduce-scatter.5.cloned.1.call-update
  274.3 126.7 %reduce-scatter.5.cloned.1.call-done = f32[256,128]{1,0:T(8,128)} async-done(((f32[8192,128]{1,0:T(8,128)}), f32[256,128]{1,0:T(8,128)}) %reduce-scatter.5.cloned.1.call-update) | async-done | bytes 131088 | tf_op jit(solution)/shard_map/reduce_scatter | solution.py:53
  401.0 1.6 fusion.4
  (3 shorter events, 0.0 us)
Async XLA Ops:
  9.0 17.1 %all-to-all-start = ((bf16[8,256,128]{2,1,0:T(8,128)(2,1)}), bf16[8,256,128]{2,1,0:T(8,128)(2,1)S(1)}, u32[]{:S(2)}, u32[]{:S(2)}) async-start(bf16[8,256,128]{2,1,0:T(8,128)(2,1)} %stack.4), calls=%async_computation | async-start | bytes 1048576 | tf_op jit(solution)/shard_map/all_to_all | solution.py:30
  14.8 194.7 %reduce-scatter.3.cloned.1.call-start = ((), (), s32[]{:S(2)}) async-start(), calls=%async_computation.4 | async-start | bytes 4325376 | tf_op jit(solution)/shard_map/reduce_scatter | solution.py:53
  19.4 6.7 %copy-start.1 = (s32[1,1,256]{2,1,0:T(1,128)S(1)}, s32[1,1,256]{2,1,0:T(1,128)}, u32[]{:S(2)}) copy-start(s32[1,1,256]{2,1,0:T(1,128)} %param.9) | copy-start | bytes 3076
  78.9 130.6 %copy-start = (bf16[256,128]{1,0:T(8,128)(2,1)S(1)}, bf16[256,128]{1,0:T(8,128)(2,1)}, u32[]{:S(2)}) copy-start(bf16[256,128]{1,0:T(8,128)(2,1)} %param.6) | copy-start | bytes 196612
  78.9 322.1 %reduce-scatter.5.cloned.1.call-start = ((), (), s32[]{:S(2)}) async-start(), calls=%async_computation.5 | async-start | bytes 4325376 | tf_op jit(solution)/shard_map/reduce_scatter | solution.py:53
Sparse Core Ops, SparseCore 0:
  79.1 130.4 reduce-scatter.2
  274.4 126.5 reduce-scatter.4
